TPU v7x, 128 devices: a whole 4x4x4 slice. The times are simulated.
128 devices in a mesh: row: 16 (over z_lo, x, core), col: 8 (over z_hi, y).
Axes of the slice: x: 4, y: 4, z: 4 (z_hi: 2, z_lo: 2; z = z_hi * 2 + z_lo), core: 2. Of those that a mesh axis runs over, the one named last changes fastest.
Arguments:
- inverse_front: float32 [16384, 16384], P('row', 'col'), may hold values from -0.09375 to 0.09375
- factor: float32 [4096, 1024], P('row'), may hold values from -1.2 to 1.2
- unit_lower: float32 [2, 512, 512], replicated, may hold values from -0.25 to 0.25
- pivot_inverse: float32 [2, 512], replicated, may hold values from 0.5 to 4
- tile_list: int32 [2, 16], replicated, may hold values from 0 to 63, as said below
- tile_valid: int32 [2, 16], replicated, may hold values from 0 to 1, as said below
Outputs:
- inverse_column: float32 [16384, 1024], P('row')
- diagonal_block: float32 [2, 512, 512], replicated
Inputs may be any that keep to these rules, and one draw needn't show every extreme that they name: `tile_list`: each row names 16 different tile rows of the front in increasing order, exactly 1 of them among each aligned group of 4 tile rows, and the last tile row is always among them. `tile_valid`: each row holds at least one 1.
All inputs are finite; a program needn't handle non-finite values.
Results may differ from a plain program's by a relative error of at most 0.0001.
Values sent between devices are 32-bit elements; how exact they have to be, the bound alone decides.
A program may use at most 192 MiB of HBM per device.

v0:
```python
import jax
import jax.numpy as jnp
from jax import lax
from jax.sharding import PartitionSpec as P

B = 256
W = 512
NS = 2
NA = 16


def from_root(block, axis, owner):
    block = jnp.where(lax.axis_index(axis) == owner, block, jnp.zeros_like(block))
    return lax.psum(block, axis)


def inner_left(left, right):
    return lax.dot_general(
        left,
        right,
        (((0,), (0,)), ((), ())),
        precision=lax.Precision.HIGHEST,
        preferred_element_type=jnp.float32,
    )


def shards(inverse_front, factor, unit_lower, pivot_inverse, tile_list, tile_valid):
    row_count = lax.axis_size("row")
    col_count = lax.axis_size("col")
    row_span, col_span = inverse_front.shape
    row_index = lax.axis_index("row")
    col_index = lax.axis_index("col")
    identity = jnp.eye(W, dtype=jnp.float32)
    inverses = [jnp.tril(unit_lower[member], -1) + identity for member in range(NS)]

    def normalize(slab):
        return jnp.concatenate(
            [
                jnp.dot(
                    slab[:, member * W : (member + 1) * W],
                    inverses[member],
                    precision=lax.Precision.HIGHEST,
                    preferred_element_type=jnp.float32,
                )
                for member in range(NS)
            ],
            axis=1,
        )

    normalized = lax.all_gather(normalize(factor), "row", axis=0, tiled=True)
    slot_tiles = normalized.reshape(NA, B, NS, W)

    def place_tiles(first, number):
        global_tile = first + jnp.arange(number, dtype=jnp.int32)
        onehot = (
            (tile_list[:, None, :] == global_tile[None, :, None]) & (tile_valid[:, None, :] > 0)
        ).astype(jnp.float32)
        placed = jnp.einsum("sta,absw->tbsw", onehot, slot_tiles, precision=lax.Precision.HIGHEST)
        return (placed.reshape(number * B, NS * W), jnp.sum(onehot, axis=2))

    row_factor, row_chosen = place_tiles(row_index * (row_span // B), row_span // B)
    col_factor, col_chosen = place_tiles(col_index * (col_span // B), col_span // B)
    row_global = row_index * row_span + jnp.arange(row_span, dtype=jnp.int32)
    col_global = col_index * col_span + jnp.arange(col_span, dtype=jnp.int32)
    lower_part = jnp.where(row_global[:, None] >= col_global[None, :], inverse_front, 0.0)
    lower_prod = jnp.dot(
        lower_part, col_factor, precision=lax.Precision.HIGHEST, preferred_element_type=jnp.float32
    )
    strict = jnp.where(row_global[:, None] > col_global[None, :], inverse_front, 0.0)
    mirror_prod = inner_left(strict, row_factor)
    row_total = lax.psum(lower_prod, "col")
    col_total = lax.psum(mirror_prod, "row")
    grid_ratio = row_count // col_count
    offset = row_index % grid_ratio * row_span
    own_piece = lax.dynamic_slice_in_dim(col_total, offset, row_span, 0)
    mirrored = from_root(own_piece, "col", row_index // grid_ratio)
    keep_rows = jnp.repeat(row_chosen, B, axis=1)
    keep_mask = jnp.repeat(keep_rows.T, W, axis=1)
    column = -(row_total + mirrored) * keep_mask
    base_block = jnp.stack(
        [
            jnp.dot(
                inverses[member].T * pivot_inverse[member][None, :],
                inverses[member],
                precision=lax.Precision.HIGHEST,
                preferred_element_type=jnp.float32,
            )
            for member in range(NS)
        ]
    )
    diag_terms = jnp.stack(
        [
            inner_left(
                row_factor[:, member * W : (member + 1) * W],
                column[:, member * W : (member + 1) * W],
            )
            for member in range(NS)
        ]
    )
    diag_total = lax.psum(diag_terms, "row")
    diagonal_block = base_block - diag_total
    return (column, diagonal_block)


def solution(mesh):
    in_specs = (P("row", "col"), P("row", None), P(), P(), P(), P())
    out_specs = (P("row", None), P())
    return jax.shard_map(shards, mesh=mesh, in_specs=in_specs, out_specs=out_specs, check_vma=False)
```

profile of v0, /device:TPU:1, one launch (start us, length us, event | category | flops | bytes accessed | tf_op | source)
XLA Modules:
  0.0 620.7 jit_solution(13033368712311143179)
XLA Ops:
  7.2 0.0 copy-start.7
  7.2 0.0 all-gather.2.cloned.1.call-start
  7.2 3.3 convolution_bitcast_fusion.1
  10.5 3.3 convolution_bitcast_fusion.2
  13.8 1.0 pad_maximum_fusion.1
  14.8 0.0 all-gather.2.cloned.1.call-update
  14.9 0.0 all-reduce.4.cloned.1.call-start
  15.0 0.0 copy-done.7
  15.0 95.2 %all-gather.2.cloned.1.call-done = f32[4096,1024]{0,1:T(8,128)} async-done(((f32[256,1024]{0,1:T(8,128)}), f32[4096,1024]{0,1:T(8,128)}) %all-gather.2.cloned.1.call-update) | async-done | bytes 16777232 | tf_op jit(solution)/shard_map/all_gather | solution.py:50
  110.2 11.0 %copy.23 = f32[128,8,16,256]{3,2,1,0:T(8,128)S(1)} copy(f32[128,8,16,256]{3,1,2,0:T(8,128)} %bitcast.71) | data formatting | bytes 33554432
  121.2 0.0 copy-start
  121.2 0.0 copy-done.5
  121.2 6.5 %fusion.57 = f32[2,256,512,4]{1,3,2,0:T(4,128)S(1)} fusion(f32[16,256,2,512]{1,0,3,2:T(8,128)S(1)} %bitcast.67, s32[2,16]{1,0:T(2,128)S(1)} %copy-done.5, pred[2,16]{1,0:T(4,128)(4,1)S(1)} %broadcast_compare_fusion, s32[4]{0:T(128)S(1)} %iota_add_fusion.3), kind=kOutput, calls=%fused_computation.60 | convolution fusion | flops 201326848 | bytes 20971696 | tf_op jit(solution)/shard_map/sta,absw->tbsw/dot_general | solution.py:58
  127.7 0.0 copy-done
  127.7 1.0 copy.25
  128.8 0.0 copy-start.2
  128.8 2.0 copy-done.2
  130.8 57.2 %fusion = f32[2048,1024]{1,0:T(8,128)} fusion(f32[1024,1024]{0,1:T(8,128)S(1)} %bitcast.72, f32[1024,2048]{1,0:T(8,128)} %param.6, s32[2048]{0:T(1024)S(1)} %iota_add_fusion, s32[1024]{0:T(1024)S(1)} %iota_add_fusion.1), kind=kOutput, calls=%fused_computation | convolution fusion | flops 25773998080 | bytes 20983808 | tf_op jit(solution)/shard_map/dot_general | solution.py:18
  188.0 0.0 all-reduce.4.cloned.1.call-update
  188.0 0.0 all-reduce.8.cloned.1.call-start
  188.1 20.3 %copy.14 = f32[16,256,2,512]{3,0,1,2:T(8,128)} copy(f32[16,256,2,512]{1,0,3,2:T(8,128)} %bitcast.68) | data formatting | bytes 33554432 | tf_op jit(solution)/shard_map/reshape | solution.py:51
  208.4 11.9 %convolution_bitcast_fusion = f32[8,256,2,512]{3,0,1,2:T(8,128)} fusion(f32[16,256,2,512]{3,0,1,2:T(8,128)} %copy.14, s32[2,16]{1,0:T(2,128)S(1)} %copy-done.5, s32[8]{0:T(128)S(1)} %iota_add_fusion.4, pred[2,16]{1,0:T(4,128)(4,1)S(1)} %broadcast_compare_fusion), kind=kOutput, calls=%fused_computation.14 | convolution fusion | flops 402653696 | bytes 25166016 | tf_op jit(solution)/shard_map/sta,absw->tbsw/dot_general | solution.py:58
  220.4 10.5 %copy.15 = f32[8,256,2,512]{1,0,3,2:T(8,128)} copy(f32[8,256,2,512]{3,0,1,2:T(8,128)} %convolution_bitcast_fusion) | data formatting | bytes 16777216 | tf_op jit(solution)/shard_map/sta,absw->tbsw/transpose | solution.py:58
  230.8 10.9 %copy.24 = f32[128,8,8,256]{3,1,2,0:T(8,128)} copy(f32[128,8,8,256]{3,2,1,0:T(8,128)} %bitcast.69) | data formatting | bytes 16777216
  241.8 87.7 %all-reduce.4.cloned.1.call-done = f32[2048,1024]{1,0:T(8,128)} async-done(((f32[2048,1024]{1,0:T(8,128)}), f32[2048,1024]{1,0:T(8,128)}) %all-reduce.4.cloned.1.call-update) | async-done | bytes 8388624 | tf_op jit(solution)/shard_map/psum | solution.py:72
  329.5 33.9 %select_add_fusion = f32[1024,1024]{1,0:T(8,128)} fusion(f32[2048,1024]{1,0:T(8,128)} %all-reduce.4.cloned.1.call-done, s32[]{:T(128)S(6)} %select_n.43, pred[]{:T(512)S(6)} %eq.40, f32[2048,1024]{0,1:T(8,128)} %bitcast.77, f32[1024,2048]{1,0:T(8,128)} %param.6, s32[2048]{0:T(1024)S(1)} %iota_add_fusion, s32[1024]{0:T(1024)S(1)} %iota_add_fusion.1), kind=kOutput, calls=%fused_computation.7 | convolution fusion | flops 25776095232 | bytes 25178116 | tf_op jit(solution)/shard_map/dot_general | solution.py:66
  363.4 0.0 all-reduce.8.cloned.1.call-update
  363.4 0.2 all-reduce.6.cloned.1.call-start
  363.6 0.2 convert_reduce_fusion
  363.8 0.1 copy.17
  363.9 1.4 broadcast_in_dim.33
  365.3 3.0 copy.26
  368.3 106.8 %all-reduce.8.cloned.1.call-done = f32[1024,1024]{1,0:T(8,128)} async-done(((f32[1024,1024]{1,0:T(8,128)}), f32[1024,1024]{1,0:T(8,128)}) %all-reduce.8.cloned.1.call-update) | async-done | bytes 4194320 | tf_op jit(solution)/shard_map/psum | solution.py:71
  475.1 4.6 negate_multiply_fusion
  479.7 0.1 copy-done.3
  479.8 3.5 fusion.35
  483.3 3.5 fusion.30
  486.8 0.0 copy-done.1
  486.8 0.0 copy-start.6
  486.8 0.0 copy-start.4
  486.8 1.5 pad_maximum_fusion
  488.3 0.0 all-reduce.6.cloned.1.call-update
  488.3 0.0 copy-done.6
  488.4 0.8 copy-done.4
  489.2 2.3 fusion.27
  491.5 3.3 fusion.24
  494.8 115.6 %all-reduce.6.cloned.1.call-done = f32[2,512,512]{2,1,0:T(8,128)} async-done(((f32[2,512,512]{2,1,0:T(8,128)}), f32[2,512,512]{2,1,0:T(8,128)}) %all-reduce.6.cloned.1.call-update) | async-done | bytes 2097168 | tf_op jit(solution)/shard_map/psum | solution.py:100
  610.4 3.7 maximum_subtract_fusion
  (11 shorter events, 0.1 us)
Async XLA Ops:
  7.2 7.8 %copy-start.7 = (s32[2,16]{1,0:T(2,128)S(1)}, s32[2,16]{1,0:T(2,128)}, u32[]{:S(2)}) copy-start(s32[2,16]{1,0:T(2,128)} %param.11) | copy-start | bytes 388
  7.2 103.1 %all-gather.2.cloned.1.call-start = ((), (), s32[]{:S(2)}) async-start(), calls=%async_computation | async-start | bytes 17825792 | tf_op jit(solution)/shard_map/all_gather | solution.py:50
  14.9 314.6 %all-reduce.4.cloned.1.call-start = ((), (), s32[]{:S(2)}) async-start(), calls=%async_computation.1 | async-start | bytes 16777216 | tf_op jit(solution)/shard_map/psum | solution.py:72
  110.2 11.0 %copy-start.5 = (s32[2,16]{1,0:T(2,128)S(1)}, s32[2,16]{1,0:T(2,128)}, u32[]{:S(2)}) copy-start(s32[2,16]{1,0:T(2,128)} %param.10) | copy-start | bytes 388
  121.2 6.5 %copy-start = (f32[128,8,16,256]{3,2,1,0:T(8,128)}, f32[128,8,16,256]{3,2,1,0:T(8,128)S(1)}, u32[]{:S(2)}) copy-start(f32[128,8,16,256]{3,2,1,0:T(8,128)S(1)} %copy.23) | copy-start | bytes 50331652
  128.8 2.1 copy-start.2
  188.0 287.1 %all-reduce.8.cloned.1.call-start = ((), (), s32[]{:S(2)}) async-start(), calls=%async_computation.3 | async-start | bytes 8388608 | tf_op jit(solution)/shard_map/psum | solution.py:71
  363.4 247.0 %all-reduce.6.cloned.1.call-start = ((), (), s32[]{:S(2)}) async-start(), calls=%async_computation.2 | async-start | bytes 4194304 | tf_op jit(solution)/shard_map/psum | solution.py:100
  475.1 4.6 copy-start.3
  479.8 7.0 %copy-start.1 = (f32[1024,1024]{1,0:T(8,128)}, f32[1024,1024]{1,0:T(8,128)S(1)}, u32[]{:S(2)}) copy-start(f32[1024,1024]{1,0:T(8,128)S(1)} %negate_multiply_fusion) | copy-start | bytes 12582916
  486.8 1.5 copy-start.6
  486.8 2.4 copy-start.4
Sparse Core Ops, SparseCore 0:
  15.0 95.2 all-gather.1
  188.1 141.3 all-reduce.3
  363.5 111.5 all-reduce.7
  488.5 121.8 all-reduce.5
where the time goes:
time: 629 us; the launch traced here: 621 us
  waiting for transfers between devices  405 us (64%)
  matrix products  129 us (21%)
  local copies, waits for them, and re-layouts  61.2 us (10%)
  between operations  14.2 us (2%)
  other arithmetic  10.9 us (2%)
    psum x1, waiting for transfers between devices, shards(): diag_total = lax.psum(diag_terms, 'row')  116 us
    psum x1, waiting for transfers between devices, shards(): row_total = lax.psum(lower_prod, 'col')  107 us
    all_gather x1, waiting for transfers between devices, shards(): normalized = lax.all_gather(normalize(factor), 'row', axis=0, tiled=True)  95.2 us
    psum x1, waiting for transfers between devices, shards(): col_total = lax.psum(mirror_prod, 'row')  87.7 us
    dot_general x3, matrix products, inner_left(): lax.dot_general(left, right, (((0,), (0,)), ((), ())), precision=lax.Prec...  64.2 us
    dot_general x1, matrix products, shards(): jnp.dot(lower_part, col_factor, precision=lax.Precision.HIGHEST, preferre...  33.9 us
    unnamed x20, local copies, waits for them, and re-layouts  28.9 us
    reshape x1, local copies, waits for them, and re-layouts, shards(): slot_tiles = normalized.reshape(NA, B, NS, W)  20.3 us
  transfers between devices with their start and end apart: 4, of which 4 were waited for; matrix products, arithmetic and copies ran while one was open for 10% of the time, Pallas kernels for 0%

commit v1 on v0

--- a/solution.py
+++ b/solution.py
@@ -7,6 +7,12 @@
 W = 512
 NS = 2
 NA = 16
+
+
+def gather_and_add(block, mesh_axis):
+    terms = lax.all_gather(block, mesh_axis, axis=0, tiled=False)
+    summed = terms.sum(axis=0)
+    return summed
 
 
 def from_root(block, axis, owner):
@@ -97,7 +103,7 @@
             for member in range(NS)
         ]
     )
-    diag_total = lax.psum(diag_terms, "row")
+    diag_total = gather_and_add(diag_terms, "row")
     diagonal_block = base_block - diag_total
     return (column, diagonal_block)
 

time: 629 us -> 689 us (1.095)
  waiting for transfers between devices: 405 us -> 453 us
  other arithmetic: 10.9 us -> 23.1 us
    all_gather x0 -> x1, waiting for transfers between devices: none -> 163 us  [gather_and_add(): terms = lax.all_gather(block, mesh_axis, axis=0, tiled=False)]
    psum x1 -> x0, waiting for transfers between devices: 116 us -> none  [shards(): diag_total = lax.psum(diag_terms, 'row')]
    reduce_sum x0 -> x1, other arithmetic: none -> 12.7 us  [gather_and_add(): summed = terms.sum(axis=0)]
  transfers between devices with their start and end apart: 4 -> 4, of which waited for: 4 -> 4; matrix products, arithmetic and copies ran while one was open for 10% -> 9% of each run, Pallas kernels for 0% -> 0%
where the time goes in v1:
time: 689 us; the launch traced here: 681 us
  waiting for transfers between devices  453 us (66%)
  matrix products  129 us (19%)
  local copies, waits for them, and re-layouts  61.2 us (9%)
  other arithmetic  23.1 us (3%)
  between operations  14.2 us (2%)
    all_gather x1, waiting for transfers between devices, gather_and_add(): terms = lax.all_gather(block, mesh_axis, axis=0, tiled=False)  163 us
    psum x1, waiting for transfers between devices, shards(): row_total = lax.psum(lower_prod, 'col')  107 us
    all_gather x1, waiting for transfers between devices, shards(): normalized = lax.all_gather(normalize(factor), 'row', axis=0, tiled=True)  95.2 us
    psum x1, waiting for transfers between devices, shards(): col_total = lax.psum(mirror_prod, 'row')  87.7 us
    dot_general x3, matrix products, inner_left(): lax.dot_general(left, right, (((0,), (0,)), ((), ())), precision=lax.Prec...  64.2 us
    dot_general x1, matrix products, shards(): jnp.dot(lower_part, col_factor, precision=lax.Precision.HIGHEST, preferre...  33.9 us
    unnamed x20, local copies, waits for them, and re-layouts  28.9 us
    reshape x1, local copies, waits for them, and re-layouts, shards(): slot_tiles = normalized.reshape(NA, B, NS, W)  20.3 us
  transfers between devices with their start and end apart: 4, of which 4 were waited for; matrix products, arithmetic and copies ran while one was open for 9% of the time, Pallas kernels for 0%

profile of v1, /device:TPU:1, one launch (start us, length us, event | category | flops | bytes accessed | tf_op | source)
XLA Modules:
  0.0 680.8 jit_solution(1517668559472173064)
XLA Ops:
  7.2 0.0 copy-start.7
  7.2 0.0 all-gather.4.cloned.1.call-start
  7.2 3.3 convolution_bitcast_fusion.1
  10.5 3.3 convolution_bitcast_fusion.2
  13.8 1.0 pad_maximum_fusion.1
  14.8 0.0 all-gather.4.cloned.1.call-update
  14.9 0.0 all-reduce.3.cloned.1.call-start
  15.0 0.0 copy-done.7
  15.0 95.2 %all-gather.4.cloned.1.call-done = f32[4096,1024]{0,1:T(8,128)} async-done(((f32[256,1024]{0,1:T(8,128)}), f32[4096,1024]{0,1:T(8,128)}) %all-gather.4.cloned.1.call-update) | async-done | bytes 16777232 | tf_op jit(solution)/shard_map/all_gather | solution.py:56
  110.2 11.0 %copy.23 = f32[128,8,16,256]{3,2,1,0:T(8,128)S(1)} copy(f32[128,8,16,256]{3,1,2,0:T(8,128)} %bitcast.73) | data formatting | bytes 33554432
  121.2 0.0 copy-start
  121.2 0.0 copy-done.5
  121.2 6.5 fusion.57
  127.7 0.0 copy-done
  127.7 1.0 copy.25
  128.8 0.0 copy-start.2
  128.8 2.0 copy-done.2
  130.8 57.2 %fusion = f32[2048,1024]{1,0:T(8,128)} fusion(f32[1024,1024]{0,1:T(8,128)S(1)} %bitcast.74, f32[1024,2048]{1,0:T(8,128)} %param.6, s32[2048]{0:T(1024)S(1)} %iota_add_fusion, s32[1024]{0:T(1024)S(1)} %iota_add_fusion.1), kind=kOutput, calls=%fused_computation | convolution fusion | flops 25773998080 | bytes 20983808 | tf_op jit(solution)/shard_map/dot_general | solution.py:24
  188.0 0.0 all-reduce.3.cloned.1.call-update
  188.0 0.0 all-reduce.5.cloned.1.call-start
  188.1 20.3 %copy.14 = f32[16,256,2,512]{3,0,1,2:T(8,128)} copy(f32[16,256,2,512]{1,0,3,2:T(8,128)} %bitcast.69) | data formatting | bytes 33554432 | tf_op jit(solution)/shard_map/reshape | solution.py:57
  208.4 11.9 %convolution_bitcast_fusion = f32[8,256,2,512]{3,0,1,2:T(8,128)} fusion(f32[16,256,2,512]{3,0,1,2:T(8,128)} %copy.14, s32[2,16]{1,0:T(2,128)S(1)} %copy-done.5, s32[8]{0:T(128)S(1)} %iota_add_fusion.4, pred[2,16]{1,0:T(4,128)(4,1)S(1)} %broadcast_compare_fusion), kind=kOutput, calls=%fused_computation.14 | convolution fusion | flops 402653696 | bytes 25166016 | tf_op jit(solution)/shard_map/sta,absw->tbsw/dot_general | solution.py:64
  220.4 10.5 %copy.15 = f32[8,256,2,512]{1,0,3,2:T(8,128)} copy(f32[8,256,2,512]{3,0,1,2:T(8,128)} %convolution_bitcast_fusion) | data formatting | bytes 16777216 | tf_op jit(solution)/shard_map/sta,absw->tbsw/transpose | solution.py:64
  230.8 10.9 %copy.24 = f32[128,8,8,256]{3,1,2,0:T(8,128)} copy(f32[128,8,8,256]{3,2,1,0:T(8,128)} %bitcast.71) | data formatting | bytes 16777216
  241.8 87.7 %all-reduce.3.cloned.1.call-done = f32[2048,1024]{1,0:T(8,128)} async-done(((f32[2048,1024]{1,0:T(8,128)}), f32[2048,1024]{1,0:T(8,128)}) %all-reduce.3.cloned.1.call-update) | async-done | bytes 8388624 | tf_op jit(solution)/shard_map/psum | solution.py:78
  329.5 33.9 %select_add_fusion = f32[1024,1024]{1,0:T(8,128)} fusion(f32[2048,1024]{1,0:T(8,128)} %all-reduce.3.cloned.1.call-done, s32[]{:T(128)S(6)} %select_n.43, pred[]{:T(512)S(6)} %eq.40, f32[2048,1024]{0,1:T(8,128)} %bitcast.79, f32[1024,2048]{1,0:T(8,128)} %param.6, s32[2048]{0:T(1024)S(1)} %iota_add_fusion, s32[1024]{0:T(1024)S(1)} %iota_add_fusion.1), kind=kOutput, calls=%fused_computation.7 | convolution fusion | flops 25776095232 | bytes 25178116 | tf_op jit(solution)/shard_map/dot_general | solution.py:72
  363.4 0.0 all-reduce.5.cloned.1.call-update
  363.4 0.2 all-gather.6.cloned.1.call-start
  363.6 0.2 convert_reduce_fusion
  363.8 0.1 copy.17
  363.9 1.4 broadcast_in_dim.33
  365.3 3.0 copy.26
  368.3 106.8 %all-reduce.5.cloned.1.call-done = f32[1024,1024]{1,0:T(8,128)} async-done(((f32[1024,1024]{1,0:T(8,128)}), f32[1024,1024]{1,0:T(8,128)}) %all-reduce.5.cloned.1.call-update) | async-done | bytes 4194320 | tf_op jit(solution)/shard_map/psum | solution.py:77
  475.1 4.6 negate_multiply_fusion
  479.7 0.1 copy-done.3
  479.8 3.5 fusion.35
  483.3 3.5 fusion.30
  486.8 0.0 copy-done.1
  486.8 0.0 copy-start.6
  486.8 0.0 copy-start.4
  486.8 1.5 pad_maximum_fusion
  488.3 0.0 all-gather.6.cloned.1.call-update
  488.4 0.8 copy-done.4
  489.2 2.3 fusion.27
  491.5 3.3 fusion.24
  494.8 163.5 %all-gather.6.cloned.1.call-done = f32[32,512,512]{2,1,0:T(8,128)} async-done(((f32[2,512,512]{2,1,0:T(8,128)}), f32[32,512,512]{2,1,0:T(8,128)}) %all-gather.6.cloned.1.call-update) | async-done | bytes 33554448 | tf_op jit(solution)/shard_map/all_gather | solution.py:13
  658.3 12.7 %reduce_sum.19 = f32[2,512,512]{2,1,0:T(8,128)S(1)} reduce(f32[16,2,512,512]{3,2,1,0:T(8,128)} %bitcast.70, f32[]{:T(128)} %constant.45.clone.1), dimensions={0}, to_apply=%region_4.5 | reduce | flops 7864320 | bytes 35651588 | tf_op jit(solution)/shard_map/reduce_sum | solution.py:14
  671.0 3.0 maximum_subtract_fusion
  (12 shorter events, 0.1 us)
Async XLA Ops:
  7.2 7.8 %copy-start.7 = (s32[2,16]{1,0:T(2,128)S(1)}, s32[2,16]{1,0:T(2,128)}, u32[]{:S(2)}) copy-start(s32[2,16]{1,0:T(2,128)} %param.11) | copy-start | bytes 388
  7.2 103.1 %all-gather.4.cloned.1.call-start = ((), (), s32[]{:S(2)}) async-start(), calls=%async_computation | async-start | bytes 17825792 | tf_op jit(solution)/shard_map/all_gather | solution.py:56
  14.9 314.6 %all-reduce.3.cloned.1.call-start = ((), (), s32[]{:S(2)}) async-start(), calls=%async_computation.1 | async-start | bytes 16777216 | tf_op jit(solution)/shard_map/psum | solution.py:78
  110.2 11.0 %copy-start.5 = (s32[2,16]{1,0:T(2,128)S(1)}, s32[2,16]{1,0:T(2,128)}, u32[]{:S(2)}) copy-start(s32[2,16]{1,0:T(2,128)} %param.10) | copy-start | bytes 388
  121.2 6.5 copy-start
  128.8 2.1 copy-start.2
  188.0 287.1 %all-reduce.5.cloned.1.call-start = ((), (), s32[]{:S(2)}) async-start(), calls=%async_computation.3 | async-start | bytes 8388608 | tf_op jit(solution)/shard_map/psum | solution.py:77
  363.4 294.9 %all-gather.6.cloned.1.call-start = ((), (), s32[]{:S(2)}) async-start(), calls=%async_computation.2 | async-start | bytes 35651584 | tf_op jit(solution)/shard_map/all_gather | solution.py:13
  475.1 4.6 copy-start.3
  479.8 7.0 %copy-start.1 = (f32[1024,1024]{1,0:T(8,128)}, f32[1024,1024]{1,0:T(8,128)S(1)}, u32[]{:S(2)}) copy-start(f32[1024,1024]{1,0:T(8,128)S(1)} %negate_multiply_fusion) | copy-start | bytes 12582916
  486.8 1.5 copy-start.6
  486.8 2.4 copy-start.4
Sparse Core Ops, SparseCore 0:
  15.0 95.2 all-gather.3
  188.1 141.3 all-reduce.2
  363.5 111.5 all-reduce.4
  488.5 169.7 all-gather.5
